TPU v7x, 32 devices: a whole 2x2x4 slice. The times are simulated.
32 devices in a mesh: fsdp: 4 (over z), ctx: 2 (over x), tp: 4 (over y, core).
Axes of the slice: x: 2, y: 2, z: 4, core: 2. Of those that a mesh axis runs over, the one named last changes fastest.
Arguments:
- tokens: bfloat16 [12288, 2048], P(('fsdp', 'ctx'), 'tp'), may hold values from -6 to 6
- cotangent: bfloat16 [12288, 2048], P(('fsdp', 'ctx'), 'tp'), may hold values from -6 to 6
- lengths: int32 [4, 6], replicated, may hold values from 1 to 1024, 3072 in all within a row
- order: int32 [24], replicated, may hold values from 0 to 23, each once
- w_query: bfloat16 [2048, 2048], P('fsdp', 'tp'), may hold values from -0.1875 to 0.1875
- w_key: bfloat16 [2048, 2048], P('fsdp', 'tp'), may hold values from -0.1875 to 0.1875
- w_value: bfloat16 [2048, 2048], P('fsdp', 'tp'), may hold values from -0.125 to 0.125
- w_output: bfloat16 [2048, 2048], P('fsdp', 'tp'), may hold values from -0.375 to 0.375
- w_gate: bfloat16 [2048, 8192], P('fsdp', 'tp'), may hold values from -0.125 to 0.125
- w_up: bfloat16 [2048, 8192], P('fsdp', 'tp'), may hold values from -0.125 to 0.125
- w_down: bfloat16 [2048, 8192], P('fsdp', 'tp'), may hold values from -0.0625 to 0.0625
Outputs:
- layer_out: bfloat16 [12288, 2048], P(('fsdp', 'ctx'), 'tp')
- input_grad: bfloat16 [12288, 2048], P(('fsdp', 'ctx'), 'tp')
- grad_query: float32 [2048, 2048], P('fsdp', 'tp')
- grad_key: float32 [2048, 2048], P('fsdp', 'tp')
- grad_value: float32 [2048, 2048], P('fsdp', 'tp')
- grad_output: float32 [2048, 2048], P('fsdp', 'tp')
- grad_gate: float32 [2048, 8192], P('fsdp', 'tp')
- grad_up: float32 [2048, 8192], P('fsdp', 'tp')
- grad_down: float32 [2048, 8192], P('fsdp', 'tp')
Inputs may be any that keep to these rules, and one draw needn't show every extreme that they name: Each row gives the lengths of the 6 sequences dealt to one index of fsdp; a row sums to the tokens of that index (1536 times the size of ctx), and its longest sequence has exactly 1024 tokens. `order`: A permutation of the sequence numbers.
All inputs are finite; a program needn't handle non-finite values.
Results may differ from a plain program's by a relative error of at most 0.019.
Values may be sent and summed in bfloat16 or wider, within the bound.
No kernel may reach another device: no remote copies, remote signals or barrier semaphores. Data moves between devices by JAX's collectives and lax.ppermute only.
A program may use at most 320 MiB of HBM per device.

v0:
```python
import math
import jax
import jax.numpy as jnp
from jax import lax
from jax.sharding import PartitionSpec as P

HD = 128
EPSILON = 1e-05
NEG_FILL = -1e30


def normalize(values):
    average = jnp.mean(values, axis=-1, keepdims=True)
    centred = values - average
    spread = jnp.mean(centred * centred, axis=-1, keepdims=True)
    inv_dev = lax.rsqrt(spread + EPSILON)
    return (centred * inv_dev, inv_dev)


def norm_back(grad, normed, inv_dev):
    grad_mean = jnp.mean(grad, axis=-1, keepdims=True)
    cross_mean = jnp.mean(grad * normed, axis=-1, keepdims=True)
    return inv_dev * (grad - grad_mean - normed * cross_mean)


def rope_tables(within):
    half_size = HD // 2
    steps_idx = jnp.arange(half_size, dtype=jnp.float32)
    freq = jnp.exp(steps_idx * (-2.0 * math.log(10000.0) / HD))
    angle = within.astype(jnp.float32)[:, None] * freq[None, :]
    angle = jnp.concatenate([angle, angle], axis=1)
    return (jnp.cos(angle)[:, None, :], jnp.sin(angle)[:, None, :])


def rotate(vector, cos_tab, sin_tab):
    half_size = vector.shape[-1] // 2
    turned = jnp.concatenate([-vector[..., half_size:], vector[..., :half_size]], axis=-1)
    return vector * cos_tab + turned * sin_tab


def rotate_back(grad, cos_tab, sin_tab):
    half_size = grad.shape[-1] // 2
    scaled = grad * sin_tab
    turned = jnp.concatenate([scaled[..., half_size:], -scaled[..., :half_size]], axis=-1)
    return grad * cos_tab + turned


def seq_tables(lengths, order):
    seq_len = lengths.reshape(-1)
    seq_ids = jnp.arange(seq_len.shape[0], dtype=jnp.int32)
    dealt_start = jnp.cumsum(seq_len) - seq_len
    picks = order[:, None] == seq_ids[None, :]
    order_len = jnp.sum(jnp.where(picks, seq_len[None, :], 0), axis=1)
    slot_start = jnp.cumsum(order_len) - order_len
    orig_start = jnp.sum(jnp.where(picks, slot_start[:, None], 0), axis=0)
    return (seq_ids, dealt_start, slot_start, orig_start)


def locate(index, starts):
    inside = index[:, None] >= starts[None, :]
    which = jnp.sum(inside.astype(jnp.int32), axis=1) - 1
    first = jnp.max(jnp.where(inside, starts[None, :], 0), axis=1)
    return (which, index - first)


def lookup(which, table, seq_ids):
    return jnp.sum(jnp.where(which[:, None] == seq_ids[None, :], table[None, :], 0), axis=1)


def tp_total(partial_value):
    return lax.psum(partial_value, "tp")


def dot_plain(left, right):
    return jnp.dot(left, right, preferred_element_type=jnp.float32)


def dot_last(left, right):
    return lax.dot_general(
        left, right, (((1,), (1,)), ((), ())), preferred_element_type=jnp.float32
    )


def dot_rows(left, right):
    return lax.dot_general(
        left, right, (((0,), (0,)), ((), ())), preferred_element_type=jnp.float32
    )


def body(
    tokens, cotangent, lengths, order, w_query, w_key, w_value, w_output, w_gate, w_up, w_down
):
    tok_rows = tokens.shape[0]
    ctx_count = lax.axis_size("ctx")
    ctx_place = lax.axis_index("ctx")
    fsdp_place = lax.axis_index("fsdp")
    tp_place = lax.axis_index("tp")
    group_rows = tok_rows * ctx_count
    block_place = fsdp_place * ctx_count + ctx_place
    scale = HD ** (-0.5)
    seq_ids, dealt_start, slot_start, orig_start = seq_tables(lengths, order)
    key_index = fsdp_place * group_rows + jnp.arange(group_rows, dtype=jnp.int32)
    key_seq, key_pos = locate(key_index, dealt_start)
    query_seq = lax.dynamic_slice_in_dim(key_seq, ctx_place * tok_rows, tok_rows)
    query_pos = lax.dynamic_slice_in_dim(key_pos, ctx_place * tok_rows, tok_rows)
    source = lookup(query_seq, orig_start, seq_ids) + query_pos
    spread_x, spread_g = (
        lax.all_gather(tokens, ("fsdp", "ctx"), axis=0, tiled=True),
        lax.all_gather(cotangent, ("fsdp", "ctx"), axis=0, tiled=True),
    )
    dealt_x = jnp.take(spread_x, source, axis=0)
    dealt_g = jnp.take(spread_g, source, axis=0)
    full_x, full_g = (
        lax.all_gather(dealt_x, "tp", axis=1, tiled=True),
        lax.all_gather(dealt_g, "tp", axis=1, tiled=True),
    )
    weights = (w_query, w_key, w_value, w_output, w_gate, w_up, w_down)
    wq_full, wk_full, wv_full, wo_full, wg_full, wu_full, wd_full = (
        lax.all_gather(weights[0], "fsdp", axis=0, tiled=True),
        lax.all_gather(weights[1], "fsdp", axis=0, tiled=True),
        lax.all_gather(weights[2], "fsdp", axis=0, tiled=True),
        lax.all_gather(weights[3], "fsdp", axis=0, tiled=True),
        lax.all_gather(weights[4], "fsdp", axis=0, tiled=True),
        lax.all_gather(weights[5], "fsdp", axis=0, tiled=True),
        lax.all_gather(weights[6], "fsdp", axis=0, tiled=True),
    )
    head_count = wq_full.shape[1] // HD
    own_cos, own_sin = rope_tables(query_pos)
    resid = full_x.astype(jnp.float32)
    normed1, inv_dev1 = normalize(resid)
    hidden1 = normed1.astype(jnp.bfloat16)
    query_rot = rotate(
        dot_plain(hidden1, wq_full).reshape(tok_rows, head_count, HD), own_cos, own_sin
    ).astype(jnp.bfloat16)
    key_rot = rotate(
        dot_plain(hidden1, wk_full).reshape(tok_rows, head_count, HD), own_cos, own_sin
    ).astype(jnp.bfloat16)
    value_low = dot_plain(hidden1, wv_full).astype(jnp.bfloat16).reshape(tok_rows, head_count, HD)
    keys_all, values_all = (
        lax.all_gather(key_rot, "ctx", axis=0, tiled=True),
        lax.all_gather(value_low, "ctx", axis=0, tiled=True),
    )
    block_rows = min(512, tok_rows)
    block_count = tok_rows // block_rows
    query_blocks = query_rot.reshape(block_count, block_rows, head_count, HD)
    seq_blocks = query_seq.reshape(block_count, block_rows)
    pos_blocks = query_pos.reshape(block_count, block_rows)

    def scores_of(query_blk, seq_blk, pos_blk):
        raw = (
            jnp.einsum("qhd,khd->hqk", query_blk, keys_all, preferred_element_type=jnp.float32)
            * scale
        )
        allowed = (seq_blk[:, None] == key_seq[None, :]) & (key_pos[None, :] <= pos_blk[:, None])
        return (raw, allowed)

    def attend(inputs):
        query_blk, seq_blk, pos_blk = inputs
        raw, allowed = scores_of(query_blk, seq_blk, pos_blk)
        masked = jnp.where(allowed[None], raw, NEG_FILL)
        top_score = jnp.max(masked, axis=-1, keepdims=True)
        expo = jnp.where(allowed[None], jnp.exp(masked - top_score), 0.0)
        denom = jnp.sum(expo, axis=-1, keepdims=True)
        probs = (expo / denom).astype(jnp.bfloat16)
        attended = jnp.einsum("hqk,khd->qhd", probs, values_all, preferred_element_type=jnp.float32)
        return (attended, top_score[..., 0] + jnp.log(denom[..., 0]))

    attended, log_norm = lax.map(attend, (query_blocks, seq_blocks, pos_blocks))
    mixed_low = attended.reshape(tok_rows, head_count * HD).astype(jnp.bfloat16)
    attn_part = dot_last(mixed_low, wo_full)
    resid1 = resid + tp_total(attn_part)
    normed2, inv_dev2 = normalize(resid1)
    hidden2 = normed2.astype(jnp.bfloat16)
    gate_proj = dot_plain(hidden2, wg_full)
    up_proj = dot_plain(hidden2, wu_full)
    sig_gate = jax.nn.sigmoid(gate_proj)
    silu_gate = gate_proj * sig_gate
    act_low = (silu_gate * up_proj).astype(jnp.bfloat16)
    mlp_full = dot_last(act_low, wd_full)
    mlp_part = lax.psum_scatter(
        mlp_full.astype(jnp.bfloat16), "tp", scatter_dimension=1, tiled=True
    ).astype(jnp.float32)
    col_count = mlp_part.shape[1]
    resid1_mine = lax.dynamic_slice_in_dim(resid1, tp_place * col_count, col_count, 1)
    y_mine = (resid1_mine + mlp_part).astype(jnp.bfloat16)
    grad_f = full_g.astype(jnp.float32)
    dact = dot_plain(full_g, wd_full).astype(jnp.bfloat16).astype(jnp.float32)
    dgate_low = (dact * up_proj * sig_gate * (1.0 + gate_proj * (1.0 - sig_gate))).astype(
        jnp.bfloat16
    )
    dup_low = (dact * silu_gate).astype(jnp.bfloat16)
    dh2_part = dot_last(dgate_low, wg_full) + dot_last(dup_low, wu_full)
    dx1 = grad_f + norm_back(tp_total(dh2_part), normed2, inv_dev2)
    da_low = dx1.astype(jnp.bfloat16)
    dout_low = dot_plain(da_low, wo_full).astype(jnp.bfloat16)
    dout_blocks = dout_low.reshape(block_count, block_rows, head_count, HD)

    def attend_back(carry, inputs):
        dk_acc, dv_acc = carry
        query_blk, seq_blk, pos_blk, lse_blk, dout_blk = inputs
        raw, allowed = scores_of(query_blk, seq_blk, pos_blk)
        probs = jnp.where(allowed[None], jnp.exp(raw - lse_blk[..., None]), 0.0)
        dprob = jnp.einsum("qhd,khd->hqk", dout_blk, values_all, preferred_element_type=jnp.float32)
        delta = jnp.sum(probs * dprob, axis=-1, keepdims=True)
        dscore = (probs * (dprob - delta)).astype(jnp.bfloat16)
        dquery = (
            jnp.einsum("hqk,khd->qhd", dscore, keys_all, preferred_element_type=jnp.float32) * scale
        )
        dk_acc = (
            dk_acc
            + jnp.einsum("hqk,qhd->khd", dscore, query_blk, preferred_element_type=jnp.float32)
            * scale
        )
        dv_acc = dv_acc + jnp.einsum(
            "hqk,qhd->khd", probs.astype(jnp.bfloat16), dout_blk, preferred_element_type=jnp.float32
        )
        return ((dk_acc, dv_acc), dquery)

    zero_keys = jnp.zeros((group_rows, head_count, HD), jnp.float32)
    (dk_all, dv_all), dq_blocks = lax.scan(
        attend_back,
        (zero_keys, zero_keys),
        (query_blocks, seq_blocks, pos_blocks, log_norm, dout_blocks),
    )
    dk_sum, dv_sum = (
        lax.psum_scatter(
            dk_all.astype(jnp.bfloat16), "ctx", scatter_dimension=0, tiled=True
        ).astype(jnp.float32),
        lax.psum_scatter(
            dv_all.astype(jnp.bfloat16), "ctx", scatter_dimension=0, tiled=True
        ).astype(jnp.float32),
    )
    width_heads = head_count * HD
    dq_low = (
        rotate_back(dq_blocks.reshape(tok_rows, head_count, HD), own_cos, own_sin)
        .astype(jnp.bfloat16)
        .reshape(tok_rows, width_heads)
    )
    dk_low = (
        rotate_back(dk_sum, own_cos, own_sin).astype(jnp.bfloat16).reshape(tok_rows, width_heads)
    )
    dv_low = dv_sum.astype(jnp.bfloat16).reshape(tok_rows, width_heads)
    dh1_part = dot_last(dq_low, wq_full) + dot_last(dk_low, wk_full) + dot_last(dv_low, wv_full)
    dx_full = dx1 + norm_back(tp_total(dh1_part), normed1, inv_dev1)
    dx_mine = lax.dynamic_slice_in_dim(dx_full, tp_place * col_count, col_count, 1).astype(
        jnp.bfloat16
    )
    orig_index = block_place * tok_rows + jnp.arange(tok_rows, dtype=jnp.int32)
    slot_which, slot_within = locate(orig_index, slot_start)
    seq_which = lookup(slot_which, order, seq_ids)
    dealt_index = lookup(seq_which, dealt_start, seq_ids) + slot_within
    back_y, back_dx = (
        lax.all_gather(y_mine, ("fsdp", "ctx"), axis=0, tiled=True),
        lax.all_gather(dx_mine, ("fsdp", "ctx"), axis=0, tiled=True),
    )
    layer_out = jnp.take(back_y, dealt_index, axis=0)
    input_grad = jnp.take(back_dx, dealt_index, axis=0)
    grads = (
        dot_rows(hidden1, dq_low),
        dot_rows(hidden1, dk_low),
        dot_rows(hidden1, dv_low),
        dot_rows(da_low, mixed_low),
        dot_rows(hidden2, dgate_low),
        dot_rows(hidden2, dup_low),
        dot_rows(full_g, act_low),
    )
    shares = (
        lax.psum_scatter(
            grads[0].astype(jnp.bfloat16), "fsdp", scatter_dimension=0, tiled=True
        ).astype(jnp.float32),
        lax.psum_scatter(
            grads[1].astype(jnp.bfloat16), "fsdp", scatter_dimension=0, tiled=True
        ).astype(jnp.float32),
        lax.psum_scatter(
            grads[2].astype(jnp.bfloat16), "fsdp", scatter_dimension=0, tiled=True
        ).astype(jnp.float32),
        lax.psum_scatter(
            grads[3].astype(jnp.bfloat16), "fsdp", scatter_dimension=0, tiled=True
        ).astype(jnp.float32),
        lax.psum_scatter(
            grads[4].astype(jnp.bfloat16), "fsdp", scatter_dimension=0, tiled=True
        ).astype(jnp.float32),
        lax.psum_scatter(
            grads[5].astype(jnp.bfloat16), "fsdp", scatter_dimension=0, tiled=True
        ).astype(jnp.float32),
        lax.psum_scatter(
            grads[6].astype(jnp.bfloat16), "fsdp", scatter_dimension=0, tiled=True
        ).astype(jnp.float32),
    )
    shares = (
        lax.psum(shares[0].astype(jnp.bfloat16), "ctx").astype(jnp.float32),
        lax.psum(shares[1].astype(jnp.bfloat16), "ctx").astype(jnp.float32),
        lax.psum(shares[2].astype(jnp.bfloat16), "ctx").astype(jnp.float32),
        lax.psum(shares[3].astype(jnp.bfloat16), "ctx").astype(jnp.float32),
        lax.psum(shares[4].astype(jnp.bfloat16), "ctx").astype(jnp.float32),
        lax.psum(shares[5].astype(jnp.bfloat16), "ctx").astype(jnp.float32),
        lax.psum(shares[6].astype(jnp.bfloat16), "ctx").astype(jnp.float32),
    )
    return (
        layer_out,
        input_grad,
        shares[0],
        shares[1],
        shares[2],
        shares[3],
        shares[4],
        shares[5],
        shares[6],
    )


def solution(mesh):
    placed = (
        P(("fsdp", "ctx"), "tp"),
        P(("fsdp", "ctx"), "tp"),
        P(),
        P(),
        P("fsdp", "tp"),
        P("fsdp", "tp"),
        P("fsdp", "tp"),
        P("fsdp", "tp"),
        P("fsdp", "tp"),
        P("fsdp", "tp"),
        P("fsdp", "tp"),
    )
    return jax.shard_map(
        body,
        mesh=mesh,
        in_specs=placed,
        out_specs=(
            P(("fsdp", "ctx"), "tp"),
            P(("fsdp", "ctx"), "tp"),
            P("fsdp", "tp"),
            P("fsdp", "tp"),
            P("fsdp", "tp"),
            P("fsdp", "tp"),
            P("fsdp", "tp"),
            P("fsdp", "tp"),
            P("fsdp", "tp"),
        ),
        check_vma=False,
    )
```

profile of v0, /device:TPU:0, one launch (start us, length us, event | category | flops | bytes accessed | tf_op | source)
XLA Modules:
  0.0 3588.8 jit_solution(7519338392230270365)
XLA Ops:
  12.8 176.6 %all-gather.40.cloned.1.call-done = bf16[12288,512]{1,0:T(8,128)(2,1)} async-done(((bf16[1536,512]{1,0:T(8,128)(2,1)}), bf16[12288,512]{1,0:T(8,128)(2,1)}) %all-gather.40.cloned.1.call-update) | async-done | bytes 12582928 | tf_op jit(solution)/shard_map/all_gather | solution.py:109
  200.4 165.8 %all-gather.16.cloned.1.call-done = bf16[12288,512]{1,0:T(8,128)(2,1)} async-done(((bf16[1536,512]{1,0:T(8,128)(2,1)}), bf16[12288,512]{1,0:T(8,128)(2,1)}) %all-gather.16.cloned.1.call-update) | async-done | bytes 12582928 | tf_op jit(solution)/shard_map/all_gather | solution.py:108
  381.4 42.8 %all-gather.18.cloned.1.call-done = bf16[1536,2048]{1,0:T(8,128)(2,1)} async-done(((bf16[1536,512]{1,0:T(8,128)(2,1)}), bf16[1536,2048]{1,0:T(8,128)(2,1)}) %all-gather.18.cloned.1.call-update) | async-done | bytes 6291472 | tf_op jit(solution)/shard_map/all_gather | solution.py:114
  435.0 36.5 %all-gather.26.cloned.1.call-done = bf16[2048,512]{1,0:T(8,128)(2,1)} async-done(((bf16[512,512]{1,0:T(8,128)(2,1)}), bf16[2048,512]{1,0:T(8,128)(2,1)}) %all-gather.26.cloned.1.call-update) | async-done | bytes 2097168 | tf_op jit(solution)/shard_map/all_gather | solution.py:121
  609.0 46.5 %all-gather.24.cloned.1.call-done = bf16[3072,4,128]{2,0,1:T(8,128)(2,1)} async-done(((bf16[1536,4,128]{2,0,1:T(8,128)(2,1)}), bf16[3072,4,128]{2,0,1:T(8,128)(2,1)}) %all-gather.24.cloned.1.call-update) | async-done | bytes 3145744 | tf_op jit(solution)/shard_map/all_gather | solution.py:140
  655.5 129.2 %while.29 = (s32[]{:T(128)}, bf16[3,512,4,128]{3,1,2,0:T(8,128)(2,1)}, f32[3,4,512]{2,1,0:T(4,128)}, s32[3,512]{1,0:T(4,128)S(1)}, s32[3072]{0:T(1024)S(1)}, /*i...) while((s32[]{:T(128)}, ...), condition=%wide.region_12.14_spmd.clone, body=%wide.region_9.13_spmd.sunk.clone | while | flops 3314022400 | bytes 114921672 | solution.py:168
  797.9 54.9 %all-gather.36.cloned.1.call-done = bf16[2048,2048]{1,0:T(8,128)(2,1)} async-done(((bf16[512,2048]{1,0:T(8,128)(2,1)}), bf16[2048,2048]{1,0:T(8,128)(2,1)}) %all-gather.36.cloned.1.call-update) | async-done | bytes 8388624 | tf_op jit(solution)/shard_map/all_gather | solution.py:125
  852.8 46.8 %all-gather.42.cloned.1.call-done = bf16[1536,2048]{1,0:T(8,128)(2,1)} async-done(((bf16[1536,512]{1,0:T(8,128)(2,1)}), bf16[1536,2048]{1,0:T(8,128)(2,1)}) %all-gather.42.cloned.1.call-update) | async-done | bytes 6291472 | tf_op jit(solution)/shard_map/all_gather | solution.py:115
  918.5 204.2 %all-reduce.6.cloned.1.call-done = f32[1536,2048]{1,0:T(8,128)} async-done(((f32[1536,2048]{1,0:T(8,128)}), f32[1536,2048]{1,0:T(8,128)}) %all-reduce.6.cloned.1.call-update) | async-done | bytes 12582928 | tf_op jit(solution)/shard_map/psum | solution.py:71
  1139.3 134.8 %all-gather.32.cloned.1.call-done = bf16[2048,2048]{1,0:T(8,128)(2,1)} async-done(((bf16[512,2048]{1,0:T(8,128)(2,1)}), bf16[2048,2048]{1,0:T(8,128)(2,1)}) %all-gather.32.cloned.1.call-update) | async-done | bytes 8388624 | tf_op jit(solution)/shard_map/all_gather | solution.py:123
  1293.0 130.4 %all-gather.34.cloned.1.call-done = bf16[2048,2048]{1,0:T(8,128)(2,1)} async-done(((bf16[512,2048]{1,0:T(8,128)(2,1)}), bf16[2048,2048]{1,0:T(8,128)(2,1)}) %all-gather.34.cloned.1.call-update) | async-done | bytes 8388624 | tf_op jit(solution)/shard_map/all_gather | solution.py:124
  1496.0 219.0 %all-reduce.8.cloned.1.call-done = f32[1536,2048]{1,0:T(8,128)} async-done(((f32[1536,2048]{1,0:T(8,128)}), f32[1536,2048]{1,0:T(8,128)}) %all-reduce.8.cloned.1.call-update) | async-done | bytes 12582928 | tf_op jit(solution)/shard_map/psum | solution.py:71
  1753.0 248.9 %while.30 = (s32[]{:T(128)}, f32[3072,4,128]{0,2,1:T(8,128)}, f32[3072,4,128]{0,2,1:T(8,128)}, f32[3,512,4,128]{3,1,2,0:T(8,128)}, bf16[3,512,4,128]{3,1,2,0:T(8...) while((s32[]{:T(128)}, f32[3072,4,128]{0,2,1:T(8,128)}, ...), condition=%wide.region_26.28_spmd.clone.clone, body=%wide.region_24.27_spmd.clone.sunk.clone | while | flops 8160278528 | bytes 277967072 | solution.py:220
  2175.9 113.2 %reduce-scatter.29.cloned.1.call-done = bf16[512,2048]{1,0:T(8,128)(2,1)} async-done(((bf16[2048,2048]{1,0:T(8,128)(2,1)}), bf16[512,2048]{1,0:T(8,128)(2,1)}) %reduce-scatter.29.cloned.1.call-update) | async-done | bytes 2097168 | tf_op jit(solution)/shard_map/reduce_scatter | solution.py:286
  2289.1 147.5 %reduce-scatter.25.cloned.1.call-done = bf16[512,2048]{1,0:T(8,128)(2,1)} async-done(((bf16[2048,2048]{1,0:T(8,128)(2,1)}), bf16[512,2048]{1,0:T(8,128)(2,1)}) %reduce-scatter.25.cloned.1.call-update) | async-done | bytes 2097168 | tf_op jit(solution)/shard_map/reduce_scatter | solution.py:280
  2436.6 147.7 %reduce-scatter.27.cloned.1.call-done = bf16[512,2048]{1,0:T(8,128)(2,1)} async-done(((bf16[2048,2048]{1,0:T(8,128)(2,1)}), bf16[512,2048]{1,0:T(8,128)(2,1)}) %reduce-scatter.27.cloned.1.call-update) | async-done | bytes 2097168 | tf_op jit(solution)/shard_map/reduce_scatter | solution.py:283
  2584.3 47.0 %reduce-scatter.21.cloned.1.call-done = bf16[512,512]{1,0:T(8,128)(2,1)} async-done(((bf16[2048,512]{1,0:T(8,128)(2,1)}), bf16[512,512]{1,0:T(8,128)(2,1)}) %reduce-scatter.21.cloned.1.call-update) | async-done | bytes 524304 | tf_op jit(solution)/shard_map/reduce_scatter | solution.py:274
  2631.3 46.1 %reduce-scatter.19.cloned.1.call-done = bf16[512,512]{1,0:T(8,128)(2,1)} async-done(((bf16[2048,512]{1,0:T(8,128)(2,1)}), bf16[512,512]{1,0:T(8,128)(2,1)}) %reduce-scatter.19.cloned.1.call-update) | async-done | bytes 524304 | tf_op jit(solution)/shard_map/reduce_scatter | solution.py:271
  2677.4 46.0 %reduce-scatter.17.cloned.1.call-done = bf16[512,512]{1,0:T(8,128)(2,1)} async-done(((bf16[2048,512]{1,0:T(8,128)(2,1)}), bf16[512,512]{1,0:T(8,128)(2,1)}) %reduce-scatter.17.cloned.1.call-update) | async-done | bytes 524304 | tf_op jit(solution)/shard_map/reduce_scatter | solution.py:268
  2723.5 60.2 %reduce-scatter.11.cloned.1.call-done = bf16[1536,512]{1,0:T(8,128)(2,1)} async-done(((bf16[1536,2048]{1,0:T(8,128)(2,1)}), bf16[1536,512]{1,0:T(8,128)(2,1)}) %reduce-scatter.11.cloned.1.call-update) | async-done | bytes 1572880 | tf_op jit(solution)/shard_map/reduce_scatter | solution.py:180
  2788.0 218.9 %all-reduce.10.cloned.1.call-done = f32[1536,2048]{1,0:T(8,128)} async-done(((f32[1536,2048]{1,0:T(8,128)}), f32[1536,2048]{1,0:T(8,128)}) %all-reduce.10.cloned.1.call-update) | async-done | bytes 12582928 | tf_op jit(solution)/shard_map/psum | solution.py:71
  3020.7 190.8 %all-reduce.12.cloned.1.call-done = (bf16[512,512]{1,0:T(8,128)(2,1)}, bf16[512,512]{1,0:T(8,128)(2,1)}, bf16[512,512]{1,0:T(8,128)(2,1)}, bf16[512,512]{1,0:T(8...) async-done(((bf16[512,512]{1,0:T(8,128)(2,1)}, bf16[512,512]{1,0:T(8,128)(2,1)}, bf16[512,512]{1,0:T(8,128)(2,1)}, ...) | async-done | bytes 8388624 | tf_op jit(solution)/shard_map/psum | solution.py:291
  3228.0 163.3 %all-gather.38.cloned.1.call-done = bf16[12288,512]{1,0:T(8,128)(2,1)} async-done(((bf16[1536,512]{1,0:T(8,128)(2,1)}), bf16[12288,512]{1,0:T(8,128)(2,1)}) %all-gather.38.cloned.1.call-update) | async-done | bytes 12582928 | tf_op jit(solution)/shard_map/all_gather | solution.py:253
  3402.3 166.6 %all-gather.44.cloned.1.call-done = bf16[12288,512]{1,0:T(8,128)(2,1)} async-done(((bf16[1536,512]{1,0:T(8,128)(2,1)}), bf16[12288,512]{1,0:T(8,128)(2,1)}) %all-gather.44.cloned.1.call-update) | async-done | bytes 12582928 | tf_op jit(solution)/shard_map/all_gather | solution.py:254
  (347 shorter events, 967.0 us)
Async XLA Ops:
  7.2 182.2 %all-gather.40.cloned.1.call-start = ((), (), s32[]{:S(2)}) async-start(), calls=%async_computation.24 | async-start | bytes 14155776 | tf_op jit(solution)/shard_map/all_gather | solution.py:109
  7.9 358.3 %all-gather.16.cloned.1.call-start = ((), (), s32[]{:S(2)}) async-start(), calls=%async_computation.10 | async-start | bytes 14155776 | tf_op jit(solution)/shard_map/all_gather | solution.py:108
  8.7 415.5 %all-gather.18.cloned.1.call-start = ((), (), s32[]{:S(2)}) async-start(), calls=%async_computation.11 | async-start | bytes 7864320 | tf_op jit(solution)/shard_map/all_gather | solution.py:114
  380.6 183.2 %all-gather.20.cloned.1.call-start = ((), (), s32[]{:S(2)}) async-start(), calls=%async_computation.12 | async-start | bytes 2621440 | tf_op jit(solution)/shard_map/all_gather | solution.py:119
  381.1 227.8 %all-gather.28.cloned.1.call-start = ((), (), s32[]{:S(2)}) async-start(), calls=%async_computation.16 | async-start | bytes 4718592 | tf_op jit(solution)/shard_map/all_gather | solution.py:141
  532.1 255.9 %all-gather.30.cloned.1.call-start = ((), (), s32[]{:S(2)}) async-start(), calls=%async_computation.17 | async-start | bytes 2621440 | tf_op jit(solution)/shard_map/all_gather | solution.py:122
  532.8 320.0 %all-gather.36.cloned.1.call-start = ((), (), s32[]{:S(2)}) async-start(), calls=%async_computation.21 | async-start | bytes 10485760 | tf_op jit(solution)/shard_map/all_gather | solution.py:125
  533.4 366.2 %all-gather.42.cloned.1.call-start = ((), (), s32[]{:S(2)}) async-start(), calls=%async_computation.25 | async-start | bytes 7864320 | tf_op jit(solution)/shard_map/all_gather | solution.py:115
  539.1 583.6 %all-reduce.6.cloned.1.call-start = ((), (), s32[]{:S(2)}) async-start(), calls=%async_computation.18 | async-start | bytes 25165824 | tf_op jit(solution)/shard_map/psum | solution.py:71
  796.5 477.6 %all-gather.32.cloned.1.call-start = ((), (), s32[]{:S(2)}) async-start(), calls=%async_computation.19 | async-start | bytes 10485760 | tf_op jit(solution)/shard_map/all_gather | solution.py:123
  797.3 626.1 %all-gather.34.cloned.1.call-start = ((), (), s32[]{:S(2)}) async-start(), calls=%async_computation.20 | async-start | bytes 10485760 | tf_op jit(solution)/shard_map/all_gather | solution.py:124
  797.9 917.1 %all-reduce.8.cloned.1.call-start = ((), (), s32[]{:S(2)}) async-start(), calls=%async_computation.26 | async-start | bytes 25165824 | tf_op jit(solution)/shard_map/psum | solution.py:71
  1495.9 585.8 %reduce-scatter.15.cloned.1.call-start = ((), (), s32[]{:S(2)}) async-start(), calls=%async_computation.28 | async-start | bytes 4718592 | tf_op jit(solution)/shard_map/reduce_scatter | solution.py:229
  2022.8 266.2 %reduce-scatter.29.cloned.1.call-start = ((), (), s32[]{:S(2)}) async-start(), calls=%async_computation.37 | async-start | bytes 10485760 | tf_op jit(solution)/shard_map/reduce_scatter | solution.py:286
  2042.5 394.1 %reduce-scatter.25.cloned.1.call-start = ((), (), s32[]{:S(2)}) async-start(), calls=%async_computation.35 | async-start | bytes 10485760 | tf_op jit(solution)/shard_map/reduce_scatter | solution.py:280
  2062.0 522.4 %reduce-scatter.27.cloned.1.call-start = ((), (), s32[]{:S(2)}) async-start(), calls=%async_computation.36 | async-start | bytes 10485760 | tf_op jit(solution)/shard_map/reduce_scatter | solution.py:283
  2081.6 549.7 %reduce-scatter.21.cloned.1.call-start = ((), (), s32[]{:S(2)}) async-start(), calls=%async_computation.33 | async-start | bytes 2621440 | tf_op jit(solution)/shard_map/reduce_scatter | solution.py:274
  2090.0 587.4 %reduce-scatter.19.cloned.1.call-start = ((), (), s32[]{:S(2)}) async-start(), calls=%async_computation.32 | async-start | bytes 2621440 | tf_op jit(solution)/shard_map/reduce_scatter | solution.py:271
  2114.0 609.4 %reduce-scatter.17.cloned.1.call-start = ((), (), s32[]{:S(2)}) async-start(), calls=%async_computation.31 | async-start | bytes 2621440 | tf_op jit(solution)/shard_map/reduce_scatter | solution.py:268
  2127.1 656.6 %reduce-scatter.11.cloned.1.call-start = ((), (), s32[]{:S(2)}) async-start(), calls=%async_computation.22 | async-start | bytes 7864320 | tf_op jit(solution)/shard_map/reduce_scatter | solution.py:180
  2146.2 860.7 %all-reduce.10.cloned.1.call-start = ((), (), s32[]{:S(2)}) async-start(), calls=%async_computation.29 | async-start | bytes 25165824 | tf_op jit(solution)/shard_map/psum | solution.py:71
  2175.8 1035.7 %all-reduce.12.cloned.1.call-start = ((), (), s32[]{:S(2)}) async-start(), calls=%async_computation.38 | async-start | bytes 16777216 | tf_op jit(solution)/shard_map/psum | solution.py:291
  2723.5 667.8 %all-gather.38.cloned.1.call-start = ((), (), s32[]{:S(2)}) async-start(), calls=%async_computation.23 | async-start | bytes 14155776 | tf_op jit(solution)/shard_map/all_gather | solution.py:253
  2787.7 781.2 %all-gather.44.cloned.1.call-start = ((), (), s32[]{:S(2)}) async-start(), calls=%async_computation.30 | async-start | bytes 14155776 | tf_op jit(solution)/shard_map/all_gather | solution.py:254
  (62 other events, 1762.9 us)
Sparse Core Ops, SparseCore 0:
  10.2 179.1 all-gather.39
  191.5 174.6 all-gather.15
  379.5 44.5 all-gather.17
  425.6 45.9 all-gather.25
  472.9 44.6 all-gather.21
  519.1 44.6 all-gather.19
  610.5 44.9 all-gather.23
  657.0 45.9 all-gather.29
  704.4 148.3 all-gather.35
  855.0 44.5 all-gather.41
  901.9 220.6 all-reduce.5
  1124.2 149.8 all-gather.31
  1275.5 147.8 all-gather.33
  1496.0 218.8 all-reduce.7
  2098.8 43.8 reduce-scatter.22
  2145.2 143.8 reduce-scatter.28
  2291.4 145.1 reduce-scatter.24
  2439.1 145.1 reduce-scatter.26
  2586.7 44.5 reduce-scatter.20
  2726.0 57.6 reduce-scatter.10
  2786.2 220.6 all-reduce.9
  3010.1 201.3 all-reduce.11
  3214.5 176.7 all-gather.37
  3394.3 174.6 all-gather.43
  (5 shorter events, 216.6 us)
where the time goes:
time: 3600 us; the launch traced here: 3590 us
  waiting for transfers between devices  2690 us (75%)
  matrix products  542 us (15%)
  other arithmetic  221 us (6%)
  local copies, waits for them, and re-layouts  117 us (3%)
    psum x3, waiting for transfers between devices, tp_total(): return lax.psum(partial_value, 'tp')  642 us
    psum x1, waiting for transfers between devices, body(): lax.psum(shares[0].astype(jnp.bfloat16), 'ctx').astype(jnp.float32)  191 us
    all_gather x1, waiting for transfers between devices, body(): lax.all_gather(cotangent, ('fsdp', 'ctx'), axis=0, tiled=True)  177 us
    all_gather x1, waiting for transfers between devices, body(): lax.all_gather(dx_mine, ('fsdp', 'ctx'), axis=0, tiled=True)  167 us
    all_gather x1, waiting for transfers between devices, body(): lax.all_gather(tokens, ('fsdp', 'ctx'), axis=0, tiled=True)  166 us
    all_gather x1, waiting for transfers between devices, body(): lax.all_gather(y_mine, ('fsdp', 'ctx'), axis=0, tiled=True)  163 us
    reduce_scatter x1, waiting for transfers between devices, body(): lax.psum_scatter(grads[5].astype(jnp.bfloat16), 'fsdp', scatter_dimension...  148 us
    reduce_scatter x1, waiting for transfers between devices, body(): lax.psum_scatter(grads[4].astype(jnp.bfloat16), 'fsdp', scatter_dimension...  148 us
  transfers between devices with their start and end apart: 29, of which 26 were waited for; matrix products, arithmetic and copies ran while one was open for 13% of the time, Pallas kernels for 0%

commit v1 on v0

--- a/solution.py
+++ b/solution.py
@@ -68,7 +68,7 @@
 
 
 def tp_total(partial_value):
-    return lax.psum(partial_value, "tp")
+    return jnp.sum(lax.all_gather(partial_value, "tp"), axis=0)
 
 
 def dot_plain(left, right):

time: 3600 us -> 3860 us (1.072)
  waiting for transfers between devices: 2690 us -> 2850 us
  other arithmetic: 221 us -> 326 us
    all_gather x0 -> x3, waiting for transfers between devices: none -> 873 us  [tp_total(): return jnp.sum(lax.all_gather(partial_value, 'tp'), axis=0)]
    psum x3 -> x0, waiting for transfers between devices: 642 us -> none  [tp_total(): return lax.psum(partial_value, 'tp')]
    reduce_sum x0 -> x5, other arithmetic: none -> 88.8 us  [the longest x3 71.5 us: tp_total(): return jnp.sum(lax.all_gather(partial_value, 'tp'), axis=0)]
    reduce_scatter x1, waiting for transfers between devices: 60.2 us -> 0.02 us  [body(): lax.psum_scatter(mlp_full.astype(jnp.bfloat16), 'tp', scatter_dimension=1...]
    reduce_scatter x1, waiting for transfers between devices: 0.02 us -> 47 us  [body(): lax.psum_scatter(grads[3].astype(jnp.bfloat16), 'fsdp', scatter_dimension...]
  transfers between devices with their start and end apart: 29 -> 29, of which waited for: 26 -> 25; matrix products, arithmetic and copies ran while one was open for 13% -> 14% of each run, Pallas kernels for 0% -> 0%
where the time goes in v1:
time: 3860 us; the launch traced here: 3850 us
  waiting for transfers between devices  2850 us (74%)
  matrix products  541 us (14%)
  other arithmetic  326 us (8%)
  local copies, waits for them, and re-layouts  118 us (3%)
    all_gather x3, waiting for transfers between devices, tp_total(): return jnp.sum(lax.all_gather(partial_value, 'tp'), axis=0)  873 us
    psum x1, waiting for transfers between devices, body(): lax.psum(shares[0].astype(jnp.bfloat16), 'ctx').astype(jnp.float32)  192 us
    all_gather x1, waiting for transfers between devices, body(): lax.all_gather(cotangent, ('fsdp', 'ctx'), axis=0, tiled=True)  177 us
    all_gather x1, waiting for transfers between devices, body(): lax.all_gather(tokens, ('fsdp', 'ctx'), axis=0, tiled=True)  166 us
    all_gather x1, waiting for transfers between devices, body(): lax.all_gather(dx_mine, ('fsdp', 'ctx'), axis=0, tiled=True)  163 us
    reduce_scatter x1, waiting for transfers between devices, body(): lax.psum_scatter(grads[5].astype(jnp.bfloat16), 'fsdp', scatter_dimension...  148 us
    reduce_scatter x1, waiting for transfers between devices, body(): lax.psum_scatter(grads[4].astype(jnp.bfloat16), 'fsdp', scatter_dimension...  148 us
    all_gather x1, waiting for transfers between devices, body(): lax.all_gather(weights[5], 'fsdp', axis=0, tiled=True)  130 us
  transfers between devices with their start and end apart: 29, of which 25 were waited for; matrix products, arithmetic and copies ran while one was open for 14% of the time, Pallas kernels for 0%

profile of v1, /device:TPU:0, one launch (start us, length us, event | category | flops | bytes accessed | tf_op | source)
XLA Modules:
  0.0 3854.5 jit_solution(17395332996017824957)
XLA Ops:
  12.8 176.5 %all-gather.46.cloned.1.call-done = bf16[12288,512]{1,0:T(8,128)(2,1)} async-done(((bf16[1536,512]{1,0:T(8,128)(2,1)}), bf16[12288,512]{1,0:T(8,128)(2,1)}) %all-gather.46.cloned.1.call-update) | async-done | bytes 12582928 | tf_op jit(solution)/shard_map/all_gather | solution.py:109
  200.4 165.8 %all-gather.22.cloned.1.call-done = bf16[12288,512]{1,0:T(8,128)(2,1)} async-done(((bf16[1536,512]{1,0:T(8,128)(2,1)}), bf16[12288,512]{1,0:T(8,128)(2,1)}) %all-gather.22.cloned.1.call-update) | async-done | bytes 12582928 | tf_op jit(solution)/shard_map/all_gather | solution.py:108
  381.4 42.7 %all-gather.24.cloned.1.call-done = bf16[1536,2048]{1,0:T(8,128)(2,1)} async-done(((bf16[1536,512]{1,0:T(8,128)(2,1)}), bf16[1536,2048]{1,0:T(8,128)(2,1)}) %all-gather.24.cloned.1.call-update) | async-done | bytes 6291472 | tf_op jit(solution)/shard_map/all_gather | solution.py:114
  435.0 36.5 all-gather.32.cloned.1.call-done
  609.0 46.5 %all-gather.30.cloned.1.call-done = bf16[3072,4,128]{2,0,1:T(8,128)(2,1)} async-done(((bf16[1536,4,128]{2,0,1:T(8,128)(2,1)}), bf16[3072,4,128]{2,0,1:T(8,128)(2,1)}) %all-gather.30.cloned.1.call-update) | async-done | bytes 3145744 | tf_op jit(solution)/shard_map/all_gather | solution.py:140
  655.5 128.9 %while.29 = (s32[]{:T(128)}, bf16[3,512,4,128]{3,1,2,0:T(8,128)(2,1)}, f32[3,4,512]{2,1,0:T(4,128)}, s32[3,512]{1,0:T(4,128)S(1)}, s32[3072]{0:T(1024)S(1)}, /*i...) while((s32[]{:T(128)}, ...), condition=%wide.region_12.14_spmd.clone, body=%wide.region_9.13_spmd.sunk.clone | while | flops 3314022400 | bytes 114921672 | solution.py:168
  797.5 55.3 %all-gather.42.cloned.1.call-done = bf16[2048,2048]{1,0:T(8,128)(2,1)} async-done(((bf16[512,2048]{1,0:T(8,128)(2,1)}), bf16[2048,2048]{1,0:T(8,128)(2,1)}) %all-gather.42.cloned.1.call-update) | async-done | bytes 8388624 | tf_op jit(solution)/shard_map/all_gather | solution.py:125
  852.8 46.8 %all-gather.48.cloned.1.call-done = bf16[1536,2048]{1,0:T(8,128)(2,1)} async-done(((bf16[1536,512]{1,0:T(8,128)(2,1)}), bf16[1536,2048]{1,0:T(8,128)(2,1)}) %all-gather.48.cloned.1.call-update) | async-done | bytes 6291472 | tf_op jit(solution)/shard_map/all_gather | solution.py:115
  918.4 279.8 %all-gather.52.cloned.1.call-done = f32[6144,2048]{1,0:T(8,128)} async-done(((f32[1536,2048]{1,0:T(8,128)}), f32[6144,2048]{1,0:T(8,128)}) %all-gather.52.cloned.1.call-update) | async-done | bytes 50331664 | tf_op jit(solution)/shard_map/all_gather | solution.py:71
  1238.9 110.5 %all-gather.38.cloned.1.call-done = bf16[2048,2048]{1,0:T(8,128)(2,1)} async-done(((bf16[512,2048]{1,0:T(8,128)(2,1)}), bf16[2048,2048]{1,0:T(8,128)(2,1)}) %all-gather.38.cloned.1.call-update) | async-done | bytes 8388624 | tf_op jit(solution)/shard_map/all_gather | solution.py:123
  1368.4 130.4 %all-gather.40.cloned.1.call-done = bf16[2048,2048]{1,0:T(8,128)(2,1)} async-done(((bf16[512,2048]{1,0:T(8,128)(2,1)}), bf16[2048,2048]{1,0:T(8,128)(2,1)}) %all-gather.40.cloned.1.call-update) | async-done | bytes 8388624 | tf_op jit(solution)/shard_map/all_gather | solution.py:124
  1569.5 295.4 %all-gather.54.cloned.1.call-done = f32[6144,2048]{1,0:T(8,128)} async-done(((f32[1536,2048]{1,0:T(8,128)}), f32[6144,2048]{1,0:T(8,128)}) %all-gather.54.cloned.1.call-update) | async-done | bytes 50331664 | tf_op jit(solution)/shard_map/all_gather | solution.py:71
  1943.4 248.8 %while.30 = (s32[]{:T(128)}, f32[3072,4,128]{0,2,1:T(8,128)}, f32[3072,4,128]{0,2,1:T(8,128)}, f32[3,512,4,128]{3,1,2,0:T(8,128)}, bf16[3,512,4,128]{3,1,2,0:T(8...) while((s32[]{:T(128)}, f32[3072,4,128]{0,2,1:T(8,128)}, ...), condition=%wide.region_26.28_spmd.clone.clone, body=%wide.region_24.27_spmd.clone.sunk.clone | while | flops 8160278528 | bytes 277967072 | solution.py:220
  2367.1 127.5 %reduce-scatter.29.cloned.1.call-done = bf16[512,2048]{1,0:T(8,128)(2,1)} async-done(((bf16[2048,2048]{1,0:T(8,128)(2,1)}), bf16[512,2048]{1,0:T(8,128)(2,1)}) %reduce-scatter.29.cloned.1.call-update) | async-done | bytes 2097168 | tf_op jit(solution)/shard_map/reduce_scatter | solution.py:286
  2494.6 147.6 %reduce-scatter.25.cloned.1.call-done = bf16[512,2048]{1,0:T(8,128)(2,1)} async-done(((bf16[2048,2048]{1,0:T(8,128)(2,1)}), bf16[512,2048]{1,0:T(8,128)(2,1)}) %reduce-scatter.25.cloned.1.call-update) | async-done | bytes 2097168 | tf_op jit(solution)/shard_map/reduce_scatter | solution.py:280
  2642.2 147.7 %reduce-scatter.27.cloned.1.call-done = bf16[512,2048]{1,0:T(8,128)(2,1)} async-done(((bf16[2048,2048]{1,0:T(8,128)(2,1)}), bf16[512,2048]{1,0:T(8,128)(2,1)}) %reduce-scatter.27.cloned.1.call-update) | async-done | bytes 2097168 | tf_op jit(solution)/shard_map/reduce_scatter | solution.py:283
  2789.9 47.0 %reduce-scatter.23.cloned.1.call-done = bf16[512,512]{1,0:T(8,128)(2,1)} async-done(((bf16[2048,512]{1,0:T(8,128)(2,1)}), bf16[512,512]{1,0:T(8,128)(2,1)}) %reduce-scatter.23.cloned.1.call-update) | async-done | bytes 524304 | tf_op jit(solution)/shard_map/reduce_scatter | solution.py:277
  2836.9 45.5 %reduce-scatter.21.cloned.1.call-done = bf16[512,512]{1,0:T(8,128)(2,1)} async-done(((bf16[2048,512]{1,0:T(8,128)(2,1)}), bf16[512,512]{1,0:T(8,128)(2,1)}) %reduce-scatter.21.cloned.1.call-update) | async-done | bytes 524304 | tf_op jit(solution)/shard_map/reduce_scatter | solution.py:274
  2882.4 46.0 %reduce-scatter.19.cloned.1.call-done = bf16[512,512]{1,0:T(8,128)(2,1)} async-done(((bf16[2048,512]{1,0:T(8,128)(2,1)}), bf16[512,512]{1,0:T(8,128)(2,1)}) %reduce-scatter.19.cloned.1.call-update) | async-done | bytes 524304 | tf_op jit(solution)/shard_map/reduce_scatter | solution.py:271
  2928.4 46.1 %reduce-scatter.17.cloned.1.call-done = bf16[512,512]{1,0:T(8,128)(2,1)} async-done(((bf16[2048,512]{1,0:T(8,128)(2,1)}), bf16[512,512]{1,0:T(8,128)(2,1)}) %reduce-scatter.17.cloned.1.call-update) | async-done | bytes 524304 | tf_op jit(solution)/shard_map/reduce_scatter | solution.py:268
  2974.6 297.9 %all-gather.56.cloned.1.call-done = f32[6144,2048]{1,0:T(8,128)} async-done(((f32[1536,2048]{1,0:T(8,128)}), f32[6144,2048]{1,0:T(8,128)}) %all-gather.56.cloned.1.call-update) | async-done | bytes 50331664 | tf_op jit(solution)/shard_map/all_gather | solution.py:71
  3326.8 125.0 %all-gather.44.cloned.1.call-done = bf16[12288,512]{1,0:T(8,128)(2,1)} async-done(((bf16[1536,512]{1,0:T(8,128)(2,1)}), bf16[12288,512]{1,0:T(8,128)(2,1)}) %all-gather.44.cloned.1.call-update) | async-done | bytes 12582928 | tf_op jit(solution)/shard_map/all_gather | solution.py:253
  3462.9 191.7 %all-reduce.3.cloned.1.call-done = (bf16[512,512]{1,0:T(8,128)(2,1)}, bf16[512,512]{1,0:T(8,128)(2,1)}, bf16[512,512]{1,0:T(8,128)(2,1)}, bf16[512,512]{1,0:T(8,...) async-done(((bf16[512,512]{1,0:T(8,128)(2,1)}, bf16[512,512]{1,0:T(8,128)(2,1)}, bf16[512,512]{1,0:T(8,128)(2,1)}, ...) | async-done | bytes 8388624 | tf_op jit(solution)/shard_map/psum | solution.py:291
  3671.1 163.3 %all-gather.50.cloned.1.call-done = bf16[12288,512]{1,0:T(8,128)(2,1)} async-done(((bf16[1536,512]{1,0:T(8,128)(2,1)}), bf16[12288,512]{1,0:T(8,128)(2,1)}) %all-gather.50.cloned.1.call-update) | async-done | bytes 12582928 | tf_op jit(solution)/shard_map/all_gather | solution.py:254
  (366 shorter events, 1066.6 us)
Async XLA Ops:
  7.2 182.2 %all-gather.46.cloned.1.call-start = ((), (), s32[]{:S(2)}) async-start(), calls=%async_computation.23 | async-start | bytes 14155776 | tf_op jit(solution)/shard_map/all_gather | solution.py:109
  7.9 358.3 %all-gather.22.cloned.1.call-start = ((), (), s32[]{:S(2)}) async-start(), calls=%async_computation.10 | async-start | bytes 14155776 | tf_op jit(solution)/shard_map/all_gather | solution.py:108
  8.7 415.5 %all-gather.24.cloned.1.call-start = ((), (), s32[]{:S(2)}) async-start(), calls=%async_computation.11 | async-start | bytes 7864320 | tf_op jit(solution)/shard_map/all_gather | solution.py:114
  380.6 183.2 %all-gather.26.cloned.1.call-start = ((), (), s32[]{:S(2)}) async-start(), calls=%async_computation.12 | async-start | bytes 2621440 | tf_op jit(solution)/shard_map/all_gather | solution.py:119
  381.1 227.8 %all-gather.34.cloned.1.call-start = ((), (), s32[]{:S(2)}) async-start(), calls=%async_computation.16 | async-start | bytes 4718592 | tf_op jit(solution)/shard_map/all_gather | solution.py:141
  532.0 255.6 %all-gather.36.cloned.1.call-start = ((), (), s32[]{:S(2)}) async-start(), calls=%async_computation.17 | async-start | bytes 2621440 | tf_op jit(solution)/shard_map/all_gather | solution.py:122
  532.8 320.0 %all-gather.42.cloned.1.call-start = ((), (), s32[]{:S(2)}) async-start(), calls=%async_computation.20 | async-start | bytes 10485760 | tf_op jit(solution)/shard_map/all_gather | solution.py:125
  533.4 366.2 %all-gather.48.cloned.1.call-start = ((), (), s32[]{:S(2)}) async-start(), calls=%async_computation.24 | async-start | bytes 7864320 | tf_op jit(solution)/shard_map/all_gather | solution.py:115
  539.0 659.2 %all-gather.52.cloned.1.call-start = ((), (), s32[]{:S(2)}) async-start(), calls=%async_computation.35 | async-start | bytes 62914560 | tf_op jit(solution)/shard_map/all_gather | solution.py:71
  796.2 553.3 %all-gather.38.cloned.1.call-start = ((), (), s32[]{:S(2)}) async-start(), calls=%async_computation.18 | async-start | bytes 10485760 | tf_op jit(solution)/shard_map/all_gather | solution.py:123
  796.9 701.8 %all-gather.40.cloned.1.call-start = ((), (), s32[]{:S(2)}) async-start(), calls=%async_computation.19 | async-start | bytes 10485760 | tf_op jit(solution)/shard_map/all_gather | solution.py:124
  797.5 1067.4 %all-gather.54.cloned.1.call-start = ((), (), s32[]{:S(2)}) async-start(), calls=%async_computation.36 | async-start | bytes 62914560 | tf_op jit(solution)/shard_map/all_gather | solution.py:71
  1569.4 723.0 %reduce-scatter.15.cloned.1.call-start = ((), (), s32[]{:S(2)}) async-start(), calls=%async_computation.26 | async-start | bytes 4718592 | tf_op jit(solution)/shard_map/reduce_scatter | solution.py:229
  2222.4 272.1 %reduce-scatter.29.cloned.1.call-start = ((), (), s32[]{:S(2)}) async-start(), calls=%async_computation.34 | async-start | bytes 10485760 | tf_op jit(solution)/shard_map/reduce_scatter | solution.py:286
  2242.0 400.2 %reduce-scatter.25.cloned.1.call-start = ((), (), s32[]{:S(2)}) async-start(), calls=%async_computation.32 | async-start | bytes 10485760 | tf_op jit(solution)/shard_map/reduce_scatter | solution.py:280
  2261.4 528.4 %reduce-scatter.27.cloned.1.call-start = ((), (), s32[]{:S(2)}) async-start(), calls=%async_computation.33 | async-start | bytes 10485760 | tf_op jit(solution)/shard_map/reduce_scatter | solution.py:283
  2281.3 555.6 %reduce-scatter.23.cloned.1.call-start = ((), (), s32[]{:S(2)}) async-start(), calls=%async_computation.31 | async-start | bytes 2621440 | tf_op jit(solution)/shard_map/reduce_scatter | solution.py:277
  2292.2 590.2 %reduce-scatter.21.cloned.1.call-start = ((), (), s32[]{:S(2)}) async-start(), calls=%async_computation.30 | async-start | bytes 2621440 | tf_op jit(solution)/shard_map/reduce_scatter | solution.py:274
  2301.7 626.7 %reduce-scatter.19.cloned.1.call-start = ((), (), s32[]{:S(2)}) async-start(), calls=%async_computation.29 | async-start | bytes 2621440 | tf_op jit(solution)/shard_map/reduce_scatter | solution.py:271
  2321.3 653.3 %reduce-scatter.17.cloned.1.call-start = ((), (), s32[]{:S(2)}) async-start(), calls=%async_computation.28 | async-start | bytes 2621440 | tf_op jit(solution)/shard_map/reduce_scatter | solution.py:268
  2333.6 939.0 %all-gather.56.cloned.1.call-start = ((), (), s32[]{:S(2)}) async-start(), calls=%async_computation.37 | async-start | bytes 62914560 | tf_op jit(solution)/shard_map/all_gather | solution.py:71
  2362.6 1089.2 %all-gather.44.cloned.1.call-start = ((), (), s32[]{:S(2)}) async-start(), calls=%async_computation.22 | async-start | bytes 14155776 | tf_op jit(solution)/shard_map/all_gather | solution.py:253
  2366.8 1287.8 %all-reduce.3.cloned.1.call-start = ((), (), s32[]{:S(2)}) async-start(), calls=%async_computation.38 | async-start | bytes 16777216 | tf_op jit(solution)/shard_map/psum | solution.py:291
  2974.6 859.8 %all-gather.50.cloned.1.call-start = ((), (), s32[]{:S(2)}) async-start(), calls=%async_computation.27 | async-start | bytes 14155776 | tf_op jit(solution)/shard_map/all_gather | solution.py:254
  (67 other events, 1296.2 us)
Sparse Core Ops, SparseCore 0:
  10.2 179.1 all-gather.45
  191.5 174.6 all-gather.21
  379.5 44.5 all-gather.23
  425.6 45.9 all-gather.31
  472.9 44.6 all-gather.27
  519.1 44.6 all-gather.25
  565.3 43.6 all-gather.33
  610.5 44.9 all-gather.29
  657.0 45.9 all-gather.35
  704.4 148.3 all-gather.41
  855.0 44.5 all-gather.47
  901.0 297.1 all-gather.51
  1199.8 149.6 all-gather.37
  1350.9 147.8 all-gather.39
  1569.5 295.3 all-gather.53
  2289.2 58.3 reduce-scatter.10
  2350.1 144.4 reduce-scatter.28
  2496.9 145.2 reduce-scatter.24
  2644.6 145.1 reduce-scatter.26
  2792.3 44.5 reduce-scatter.22
  2976.0 296.4 all-gather.55
  3275.4 176.4 all-gather.43
  3455.2 199.3 all-reduce.2
  3657.6 176.7 all-gather.49
  (5 shorter events, 216.0 us)
